TPU v7x, 32 devices: a whole 2x2x4 slice. The times are simulated.
32 devices in a mesh: gx: 8 (over z, y), gy: 4 (over x, core).
Axes of the slice: x: 2, y: 2, z: 4, core: 2. Of those that a mesh axis runs over, the one named last changes fastest.
Arguments:
- fuel: float32 [16, 768, 384], P('gx', 'gy'), may hold values from -41 to 41, as said below
- oxidizer: float32 [16, 768, 384], P('gx', 'gy'), may hold values from -41 to 41, as said below
- kappa: float32 [16, 768, 384], P('gx', 'gy'), may hold values from 0.05 to 0.5
- rate: float32 [16, 768, 384], P('gx', 'gy'), may hold values from 0.5 to 5
Outputs:
- fuel_next: float32 [16, 768, 384], P('gx', 'gy')
- oxid_next: float32 [16, 768, 384], P('gx', 'gy')
- r_factor: float32 [384, 384], replicated
Inputs may be any that keep to these rules, and one draw needn't show every extreme that they name: `fuel`: A real-valued field. `oxidizer`: A real-valued field.
All inputs are finite; a program needn't handle non-finite values.
Results may differ from a plain program's by a relative error of at most 0.000067.
Values sent between devices are 32-bit elements; how exact they have to be, the bound alone decides.
A program may use at most 64 MiB of HBM per device.

v0:
```python
import jax
import jax.numpy as jnp
from jax import lax
from jax.sharding import PartitionSpec as P


def extended(cells, sides, width):
    for axis, dim in sides:
        count = lax.axis_size(axis)
        ends = count - 1
        head = lax.slice_in_dim(cells, 0, width, axis=dim)
        tail = lax.slice_in_dim(cells, cells.shape[dim] - width, cells.shape[dim], axis=dim)
        cells = jnp.concatenate(
            [
                lax.ppermute(tail, axis, [(i, (i + 1) % count) for i in range(ends)]),
                cells,
                lax.ppermute(head, axis, [((i + 1) % count, i) for i in range(ends)]),
            ],
            axis=dim,
        )
    return cells


def diffuse_local(padded, kpad):
    planes = padded.shape[0] - 2
    width = padded.shape[1] - 2
    total = jnp.zeros((planes, width, padded.shape[2] - 2), jnp.float32)
    center = padded[1:-1, 1:-1, 1:-1]
    kcenter = kpad[1:-1, 1:-1, 1:-1]
    sizes = (planes, width, padded.shape[2] - 2)
    for axis in range(3):
        for offset in (0, 2):
            index = [slice(1, -1)] * 3
            index[axis] = slice(offset, offset + sizes[axis])
            index = tuple(index)
            total = total + 0.5 * (kcenter + kpad[index]) * (padded[index] - center)
    return total


def local_gram(first, second):
    flat_a = first.reshape(-1, first.shape[2])
    flat_b = second.reshape(-1, second.shape[2])
    dims = (((0,), (0,)), ((), ()))
    gram = lax.dot_general(flat_a, flat_a, dims, precision=lax.Precision.HIGHEST)
    return gram + lax.dot_general(flat_b, flat_b, dims, precision=lax.Precision.HIGHEST)


def shards(fuel, oxidizer, kappa, rate):
    stacked = jnp.stack([fuel, oxidizer, kappa])
    widened = extended(stacked, (("gx", 1), ("gy", 2)), 1)
    widened = jnp.pad(widened, ((0, 0), (0, 0), (0, 0), (1, 1)))
    prod = fuel * oxidizer
    react = rate * prod / jnp.sqrt(1.0 + prod * prod)
    fuel_next = fuel + 0.15 * (diffuse_local(widened[0], widened[2]) - react)
    oxid_next = oxidizer + 0.15 * (diffuse_local(widened[1], widened[2]) + react)
    rows = 2 * fuel.shape[0] * fuel.shape[1] * lax.axis_size("gx") * lax.axis_size("gy")
    gram = local_gram(fuel_next, oxid_next) / rows
    total = lax.psum(gram, ("gx", "gy"))
    factor = jnp.linalg.cholesky(total).T
    return (fuel_next, oxid_next, factor)


def solution(mesh):
    in_specs = (P("gx", "gy", None), P("gx", "gy", None), P("gx", "gy", None), P("gx", "gy", None))
    out_specs = (P("gx", "gy", None), P("gx", "gy", None), P())
    return jax.shard_map(shards, mesh=mesh, in_specs=in_specs, out_specs=out_specs, check_vma=False)
```

profile of v0, /device:TPU:0, one launch (start us, length us, event | category | flops | bytes accessed | tf_op | source)
XLA Modules:
  0.0 272.9 jit_solution(1757577690455986732)
XLA Ops:
  7.2 0.0 copy-start.1
  7.2 0.0 copy-start
  7.2 0.0 copy-start.2
  7.2 0.0 all-reduce.4.cloned.1.call-start
  7.2 1.7 pad_maximum_fusion
  8.9 0.1 fusion.45
  9.0 5.0 %collective-permute-start = (f32[3,1,192,384]{3,2,1,0:T(8,128)S(1)}, f32[3,1,192,384]{3,2,1,0:T(8,128)S(1)}, u32[]{:S(2)}, u32[]{:S(2)}) collective-permute-start(f32[3,1,192,384]{3,2,1,0:T(8,128)S(1)} %get-tuple-element.11), channel_id=1, source_target_pairs={{0,4},{4,8},{8,12},{12,16},{16,20},{20,24},{24,28},{1,5},{5,9},{9,... | collective-permute-start | bytes 2654216 | tf_op jit(solution)/shard_map/ppermute | solution.py:15
  14.0 1.3 collective-permute-start.1
  15.3 36.5 %collective-permute-done = f32[3,1,192,384]{3,2,1,0:T(8,128)S(1)} collective-permute-done((f32[3,1,192,384]{3,2,1,0:T(8,128)S(1)}, f32[3,1,192,384]{3,2,1,0:T(8,128)S(1)}, u32[]{:S(2)}, u32[]{:S(2)}) %collective-permute-start) | collective-permute-done | bytes 884768 | tf_op jit(solution)/shard_map/ppermute | solution.py:15
  51.8 0.0 collective-permute-done.1
  51.8 0.0 copy-done.1
  51.8 0.0 copy-done
  51.8 0.0 copy-done.2
  51.8 1.3 collective-permute-start.2
  53.1 1.3 collective-permute-start.3
  54.4 0.0 collective-permute-done.2
  54.4 3.5 %collective-permute-done.3 = f32[3,4,1,384]{3,2,1,0:T(1,128)S(1)} collective-permute-done((f32[3,4,1,384]{3,2,1,0:T(1,128)S(1)}, f32[3,4,1,384]{3,2,1,0:T(1,128)S(1)}, u32[]{:S(2)}, u32[]{:S(2)}) %collective-permute-start.3) | collective-permute-done | bytes 18464 | tf_op jit(solution)/shard_map/ppermute | solution.py:17
  57.9 4.8 %select_maximum_fusion = f32[3,4,194,386]{3,2,1,0:T(8,128)S(1)} fusion(f32[3,4,1,384]{3,2,1,0:T(1,128)S(1)} %collective-permute-done.3, f32[3,4,1,384]{3,2,1,0:T(1,128)S(1)} %collective-permute-done.2, f32[3,1,192,384]{3,2,1,0:T(8,128)S(1)} %collective-permute-done.1, f32[3,1,192,384]{3,2,1,0:T(8,128)S(1)} %collective-permute-done, ...), kind=kLoop, calls=%fused_computation.2 | loop fusion | flops 14377728 | bytes 7170240 | tf_op jit(solution)/shard_map/concatenate | solution.py:13
  62.7 0.0 copy-start.5
  62.7 0.5 slice_bitcast_fusion
  63.3 0.5 copy-done.5
  63.8 2.0 fusion.7
  65.8 0.0 copy-start.3
  65.8 2.0 fusion.21
  67.9 0.0 copy-done.3
  67.9 0.0 copy-start.4
  67.9 1.4 convolution_bitcast_fusion
  69.3 2.2 fusion.2
  71.5 0.0 all-reduce.4.cloned.1.call-update
  71.5 131.7 %all-reduce.4.cloned.1.call-done = f32[384,384]{0,1:T(8,128)} async-done(((f32[384,384]{0,1:T(8,128)}), f32[384,384]{0,1:T(8,128)}) %all-reduce.4.cloned.1.call-update) | async-done | bytes 589840 | tf_op jit(solution)/shard_map/psum | solution.py:58
  203.2 1.3 copy.9
  204.5 1.1 fusion.37
  205.6 11.7 %cholesky.77 = f32[128,128]{1,0:T(8,128)S(1)} custom-call(f32[128,128]{1,0:T(8,128)S(1)} %cholesky.192), custom_call_target="Cholesky" | custom-call | tf_op jit(solution)/shard_map/jit(cholesky)/cholesky | solution.py:59
  217.4 10.0 %custom-call.19 = f32[1,128,128]{1,2,0:T(8,128)S(1)} custom-call(f32[1,128,128]{2,1,0:T(8,128)S(1)} %get-tuple-element.19), custom_call_target="InvertDiagBlocksLowerTriangular" | custom-call | tf_op jit(solution)/shard_map/jit(cholesky)/cholesky | solution.py:59
  227.4 0.3 constant_dynamic-update-slice_fusion.1
  227.7 0.3 convolution_subtract_fusion
  228.0 11.7 %cholesky.162 = f32[128,128]{1,0:T(8,128)S(1)} custom-call(f32[128,128]{1,0:T(8,128)S(1)} %cholesky.196), custom_call_target="Cholesky" | custom-call | tf_op jit(solution)/shard_map/jit(cholesky)/cholesky | solution.py:59
  239.7 0.0 copy-done.4
  239.7 9.8 %custom-call.20 = f32[1,128,128]{1,2,0:T(8,128)S(1)} custom-call(f32[1,128,128]{2,1,0:T(8,128)S(1)} %get-tuple-element.16), custom_call_target="InvertDiagBlocksLowerTriangular" | custom-call | tf_op jit(solution)/shard_map/jit(cholesky)/cholesky | solution.py:59
  249.5 0.2 convolution_dynamic-update-slice_fusion
  249.7 0.3 convolution_subtract_fusion.1
  250.0 11.7 %cholesky.181 = f32[128,128]{1,0:T(8,128)S(1)} custom-call(f32[128,128]{1,0:T(8,128)S(1)} %convolution_subtract_fusion.1), custom_call_target="Cholesky" | custom-call | tf_op jit(solution)/shard_map/jit(cholesky)/cholesky | solution.py:59
  261.8 0.6 compare_reduce_fusion
  262.4 0.7 compare_reduce_fusion.1
  265.0 1.1 copy.10
  (8 shorter events, 0.2 us)
Async XLA Ops:
  7.2 44.6 %copy-start.1 = (f32[2,192,384]{2,1,0:T(8,128)S(1)}, f32[2,192,384]{2,1,0:T(8,128)}, u32[]{:S(2)}) copy-start(f32[2,192,384]{2,1,0:T(8,128)} %param.5) | copy-start | bytes 1769476
  7.2 44.6 %copy-start = (f32[2,192,384]{2,1,0:T(8,128)S(1)}, f32[2,192,384]{2,1,0:T(8,128)}, u32[]{:S(2)}) copy-start(f32[2,192,384]{2,1,0:T(8,128)} %param.4) | copy-start | bytes 1769476
  7.2 44.6 %copy-start.2 = (f32[2,192,384]{2,1,0:T(8,128)S(1)}, f32[2,192,384]{2,1,0:T(8,128)}, u32[]{:S(2)}) copy-start(f32[2,192,384]{2,1,0:T(8,128)} %param.6) | copy-start | bytes 1769476
  7.2 196.0 %all-reduce.4.cloned.1.call-start = ((), (), s32[]{:S(2)}) async-start(), calls=%async_computation | async-start | bytes 1179648 | tf_op jit(solution)/shard_map/psum | solution.py:58
  9.0 42.8 %collective-permute-start = (f32[3,1,192,384]{3,2,1,0:T(8,128)S(1)}, f32[3,1,192,384]{3,2,1,0:T(8,128)S(1)}, u32[]{:S(2)}, u32[]{:S(2)}) collective-permute-start(f32[3,1,192,384]{3,2,1,0:T(8,128)S(1)} %get-tuple-element.11), channel_id=1, source_target_pairs={{0,4},{4,8},{8,12},{12,16},{16,20},{20,24},{24,28},{1,5},{5,9},{9,... | collective-permute-start | bytes 2654216 | tf_op jit(solution)/shard_map/ppermute | solution.py:15
  14.0 37.8 %collective-permute-start.1 = (f32[3,1,192,384]{3,2,1,0:T(8,128)S(1)}, f32[3,1,192,384]{3,2,1,0:T(8,128)S(1)}, u32[]{:S(2)}, u32[]{:S(2)}) collective-permute-start(f32[3,1,192,384]{3,2,1,0:T(8,128)S(1)} %get-tuple-element.12), channel_id=1, source_target_pairs={{4,0},{8,4},{12,8},{16,12},{20,16},{24,20},{28,24},{5,1},{9,5},{13... | collective-permute-start | bytes 2654216 | tf_op jit(solution)/shard_map/ppermute | solution.py:17
  51.8 2.6 collective-permute-start.2
  53.1 4.8 %collective-permute-start.3 = (f32[3,4,1,384]{3,2,1,0:T(1,128)S(1)}, f32[3,4,1,384]{3,2,1,0:T(1,128)S(1)}, u32[]{:S(2)}, u32[]{:S(2)}) collective-permute-start(f32[3,4,1,384]{3,2,1,0:T(1,128)S(1)} %get-tuple-element.10), channel_id=1, source_target_pairs={{1,0},{2,1},{3,2},{5,4},{6,5},{7,6},{9,8},{10,9},{11,10},{13,12},{... | collective-permute-start | bytes 55304 | tf_op jit(solution)/shard_map/ppermute | solution.py:17
  62.7 1.1 copy-start.5
  65.8 2.1 copy-start.3
  67.9 171.8 %copy-start.4 = (f32[2,192,384]{2,1,0:T(8,128)}, f32[2,192,384]{2,1,0:T(8,128)S(1)}, u32[]{:S(2)}) copy-start(f32[2,192,384]{2,1,0:T(8,128)S(1)} %fusion.21) | copy-start | bytes 1769476
Sparse Core Ops, SparseCore 0:
  71.6 131.5 all-reduce.3
where the time goes:
time: 273 us
  waiting for transfers between devices  172 us (63%)
  other arithmetic  68 us (25%)
  between operations  16.1 us (6%)
  starting transfers between devices  8.87 us (3%)
  matrix products  4.56 us (2%)
  local copies, waits for them, and re-layouts  3.59 us (1%)
    psum x1, waiting for transfers between devices, shards(): total = lax.psum(gram, ('gx', 'gy'))  132 us
    another operation x10, other arithmetic, shards(): factor = jnp.linalg.cholesky(total).T  56.3 us
    ppermute x2, waiting for transfers between devices, extended(): lax.ppermute(tail, axis, [(i, (i + 1) % count) for i in range(ends)])  36.5 us
    ppermute x2, starting transfers between devices, extended(): lax.ppermute(tail, axis, [(i, (i + 1) % count) for i in range(ends)])  6.25 us
  transfers between devices with their start and end apart: 5, of which 3 were waited for; matrix products, arithmetic and copies ran while one was open for 0% of the time, Pallas kernels for 0%

commit v1 on v0

--- a/solution.py
+++ b/solution.py
@@ -55,7 +55,7 @@
     oxid_next = oxidizer + 0.15 * (diffuse_local(widened[1], widened[2]) + react)
     rows = 2 * fuel.shape[0] * fuel.shape[1] * lax.axis_size("gx") * lax.axis_size("gy")
     gram = local_gram(fuel_next, oxid_next) / rows
-    total = lax.psum(gram, ("gx", "gy"))
+    total = lax.psum(lax.psum(gram, "gy"), "gx")
     factor = jnp.linalg.cholesky(total).T
     return (fuel_next, oxid_next, factor)
 

time: 273 us -> 255 us (0.934)
  waiting for transfers between devices: 172 us -> 154 us
    psum x1 -> x2, waiting for transfers between devices: 132 us -> 114 us  [shards(): total = lax.psum(lax.psum(gram, 'gy'), 'gx')]
  transfers between devices with their start and end apart: 5 -> 6, of which waited for: 3 -> 4; matrix products, arithmetic and copies ran while one was open for 0% -> 0% of each run, Pallas kernels for 0% -> 0%
where the time goes in v1:
time: 255 us
  waiting for transfers between devices  154 us (60%)
  other arithmetic  67.9 us (27%)
  between operations  16.1 us (6%)
  starting transfers between devices  9.09 us (4%)
  matrix products  4.54 us (2%)
  local copies, waits for them, and re-layouts  3.59 us (1%)
    psum x2, waiting for transfers between devices, shards(): total = lax.psum(lax.psum(gram, 'gy'), 'gx')  114 us
    another operation x10, other arithmetic, shards(): factor = jnp.linalg.cholesky(total).T  56.4 us
    ppermute x2, waiting for transfers between devices, extended(): lax.ppermute(tail, axis, [(i, (i + 1) % count) for i in range(ends)])  36.5 us
    ppermute x2, starting transfers between devices, extended(): lax.ppermute(tail, axis, [(i, (i + 1) % count) for i in range(ends)])  6.25 us
  transfers between devices with their start and end apart: 6, of which 4 were waited for; matrix products, arithmetic and copies ran while one was open for 0% of the time, Pallas kernels for 0%

profile of v1, /device:TPU:0, one launch (start us, length us, event | category | flops | bytes accessed | tf_op | source)
XLA Modules:
  0.0 254.9 jit_solution(8324672264682265762)
XLA Ops:
  7.2 0.0 copy-start.1
  7.2 0.0 copy-start
  7.2 0.0 copy-start.2
  7.2 0.0 all-reduce.5.cloned.1.call-start
  7.2 1.7 pad_maximum_fusion
  8.9 0.1 fusion.45
  9.0 5.0 %collective-permute-start = (f32[3,1,192,384]{3,2,1,0:T(8,128)S(1)}, f32[3,1,192,384]{3,2,1,0:T(8,128)S(1)}, u32[]{:S(2)}, u32[]{:S(2)}) collective-permute-start(f32[3,1,192,384]{3,2,1,0:T(8,128)S(1)} %get-tuple-element.11), channel_id=1, source_target_pairs={{0,4},{4,8},{8,12},{12,16},{16,20},{20,24},{24,28},{1,5},{5,9},{9,... | collective-permute-start | bytes 2654216 | tf_op jit(solution)/shard_map/ppermute | solution.py:15
  14.0 1.3 collective-permute-start.1
  15.3 36.5 %collective-permute-done = f32[3,1,192,384]{3,2,1,0:T(8,128)S(1)} collective-permute-done((f32[3,1,192,384]{3,2,1,0:T(8,128)S(1)}, f32[3,1,192,384]{3,2,1,0:T(8,128)S(1)}, u32[]{:S(2)}, u32[]{:S(2)}) %collective-permute-start) | collective-permute-done | bytes 884768 | tf_op jit(solution)/shard_map/ppermute | solution.py:15
  51.8 0.0 collective-permute-done.1
  51.8 0.0 copy-done.1
  51.8 0.0 copy-done
  51.8 0.0 copy-done.2
  51.8 1.3 collective-permute-start.2
  53.1 1.3 collective-permute-start.3
  54.4 0.0 collective-permute-done.2
  54.4 3.5 %collective-permute-done.3 = f32[3,4,1,384]{3,2,1,0:T(1,128)S(1)} collective-permute-done((f32[3,4,1,384]{3,2,1,0:T(1,128)S(1)}, f32[3,4,1,384]{3,2,1,0:T(1,128)S(1)}, u32[]{:S(2)}, u32[]{:S(2)}) %collective-permute-start.3) | collective-permute-done | bytes 18464 | tf_op jit(solution)/shard_map/ppermute | solution.py:17
  57.9 4.6 %select_maximum_fusion = f32[3,4,194,386]{3,2,1,0:T(8,128)S(1)} fusion(f32[3,4,1,384]{3,2,1,0:T(1,128)S(1)} %collective-permute-done.3, f32[3,4,1,384]{3,2,1,0:T(1,128)S(1)} %collective-permute-done.2, f32[3,1,192,384]{3,2,1,0:T(8,128)S(1)} %collective-permute-done.1, f32[3,1,192,384]{3,2,1,0:T(8,128)S(1)} %collective-permute-done, ...), kind=kLoop, calls=%fused_computation.2 | loop fusion | flops 14377728 | bytes 7170240 | tf_op jit(solution)/shard_map/concatenate | solution.py:13
  62.5 0.0 copy-start.5
  62.5 0.5 slice_bitcast_fusion
  63.1 0.5 copy-done.5
  63.6 2.0 fusion.7
  65.6 0.0 copy-start.3
  65.7 2.0 fusion.21
  67.7 0.0 copy-done.3
  67.7 0.0 copy-start.4
  67.7 1.4 convolution_bitcast_fusion
  69.1 2.1 fusion.2
  71.3 0.0 all-reduce.5.cloned.1.call-update
  71.3 0.2 all-reduce.7.cloned.1.call-start
  71.5 37.0 %all-reduce.5.cloned.1.call-done = f32[384,384]{0,1:T(8,128)} async-done(((f32[384,384]{0,1:T(8,128)}), f32[384,384]{0,1:T(8,128)}) %all-reduce.5.cloned.1.call-update) | async-done | bytes 589840 | tf_op jit(solution)/shard_map/psum | solution.py:58
  108.6 0.0 all-reduce.7.cloned.1.call-update
  108.6 76.6 %all-reduce.7.cloned.1.call-done = f32[384,384]{0,1:T(8,128)} async-done(((f32[384,384]{0,1:T(8,128)}), f32[384,384]{0,1:T(8,128)}) %all-reduce.7.cloned.1.call-update) | async-done | bytes 589840 | tf_op jit(solution)/shard_map/psum | solution.py:58
  185.2 1.3 copy.9
  186.5 1.1 fusion.37
  187.6 11.7 %cholesky.77 = f32[128,128]{1,0:T(8,128)S(1)} custom-call(f32[128,128]{1,0:T(8,128)S(1)} %cholesky.192), custom_call_target="Cholesky" | custom-call | tf_op jit(solution)/shard_map/jit(cholesky)/cholesky | solution.py:59
  199.4 9.8 %custom-call.19 = f32[1,128,128]{1,2,0:T(8,128)S(1)} custom-call(f32[1,128,128]{2,1,0:T(8,128)S(1)} %get-tuple-element.19), custom_call_target="InvertDiagBlocksLowerTriangular" | custom-call | tf_op jit(solution)/shard_map/jit(cholesky)/cholesky | solution.py:59
  209.2 0.3 constant_dynamic-update-slice_fusion.1
  209.5 0.3 convolution_subtract_fusion
  209.8 0.0 copy-done.4
  209.8 11.7 %cholesky.162 = f32[128,128]{1,0:T(8,128)S(1)} custom-call(f32[128,128]{1,0:T(8,128)S(1)} %cholesky.196), custom_call_target="Cholesky" | custom-call | tf_op jit(solution)/shard_map/jit(cholesky)/cholesky | solution.py:59
  221.6 10.0 %custom-call.20 = f32[1,128,128]{1,2,0:T(8,128)S(1)} custom-call(f32[1,128,128]{2,1,0:T(8,128)S(1)} %get-tuple-element.16), custom_call_target="InvertDiagBlocksLowerTriangular" | custom-call | tf_op jit(solution)/shard_map/jit(cholesky)/cholesky | solution.py:59
  231.6 0.2 convolution_dynamic-update-slice_fusion
  231.8 0.3 convolution_subtract_fusion.1
  232.1 11.7 %cholesky.181 = f32[128,128]{1,0:T(8,128)S(1)} custom-call(f32[128,128]{1,0:T(8,128)S(1)} %convolution_subtract_fusion.1), custom_call_target="Cholesky" | custom-call | tf_op jit(solution)/shard_map/jit(cholesky)/cholesky | solution.py:59
  243.8 0.6 compare_reduce_fusion
  244.4 0.7 compare_reduce_fusion.1
  247.0 1.1 copy.10
  (8 shorter events, 0.2 us)
Async XLA Ops:
  7.2 44.6 %copy-start.1 = (f32[2,192,384]{2,1,0:T(8,128)S(1)}, f32[2,192,384]{2,1,0:T(8,128)}, u32[]{:S(2)}) copy-start(f32[2,192,384]{2,1,0:T(8,128)} %param.5) | copy-start | bytes 1769476
  7.2 44.6 %copy-start = (f32[2,192,384]{2,1,0:T(8,128)S(1)}, f32[2,192,384]{2,1,0:T(8,128)}, u32[]{:S(2)}) copy-start(f32[2,192,384]{2,1,0:T(8,128)} %param.4) | copy-start | bytes 1769476
  7.2 44.6 %copy-start.2 = (f32[2,192,384]{2,1,0:T(8,128)S(1)}, f32[2,192,384]{2,1,0:T(8,128)}, u32[]{:S(2)}) copy-start(f32[2,192,384]{2,1,0:T(8,128)} %param.6) | copy-start | bytes 1769476
  7.2 101.4 %all-reduce.5.cloned.1.call-start = ((), (), s32[]{:S(2)}) async-start(), calls=%async_computation | async-start | bytes 1179648 | tf_op jit(solution)/shard_map/psum | solution.py:58
  9.0 42.8 %collective-permute-start = (f32[3,1,192,384]{3,2,1,0:T(8,128)S(1)}, f32[3,1,192,384]{3,2,1,0:T(8,128)S(1)}, u32[]{:S(2)}, u32[]{:S(2)}) collective-permute-start(f32[3,1,192,384]{3,2,1,0:T(8,128)S(1)} %get-tuple-element.11), channel_id=1, source_target_pairs={{0,4},{4,8},{8,12},{12,16},{16,20},{20,24},{24,28},{1,5},{5,9},{9,... | collective-permute-start | bytes 2654216 | tf_op jit(solution)/shard_map/ppermute | solution.py:15
  14.0 37.8 %collective-permute-start.1 = (f32[3,1,192,384]{3,2,1,0:T(8,128)S(1)}, f32[3,1,192,384]{3,2,1,0:T(8,128)S(1)}, u32[]{:S(2)}, u32[]{:S(2)}) collective-permute-start(f32[3,1,192,384]{3,2,1,0:T(8,128)S(1)} %get-tuple-element.12), channel_id=1, source_target_pairs={{4,0},{8,4},{12,8},{16,12},{20,16},{24,20},{28,24},{5,1},{9,5},{13... | collective-permute-start | bytes 2654216 | tf_op jit(solution)/shard_map/ppermute | solution.py:17
  51.8 2.6 %collective-permute-start.2 = (f32[3,4,1,384]{3,2,1,0:T(1,128)S(1)}, f32[3,4,1,384]{3,2,1,0:T(1,128)S(1)}, u32[]{:S(2)}, u32[]{:S(2)}) collective-permute-start(f32[3,4,1,384]{3,2,1,0:T(1,128)S(1)} %get-tuple-element.9), channel_id=1, source_target_pairs={{0,1},{1,2},{2,3},{4,5},{5,6},{6,7},{8,9},{9,10},{10,11},{12,13},{... | collective-permute-start | bytes 55304 | tf_op jit(solution)/shard_map/ppermute | solution.py:15
  53.1 4.8 %collective-permute-start.3 = (f32[3,4,1,384]{3,2,1,0:T(1,128)S(1)}, f32[3,4,1,384]{3,2,1,0:T(1,128)S(1)}, u32[]{:S(2)}, u32[]{:S(2)}) collective-permute-start(f32[3,4,1,384]{3,2,1,0:T(1,128)S(1)} %get-tuple-element.10), channel_id=1, source_target_pairs={{1,0},{2,1},{3,2},{5,4},{6,5},{7,6},{9,8},{10,9},{11,10},{13,12},{... | collective-permute-start | bytes 55304 | tf_op jit(solution)/shard_map/ppermute | solution.py:17
  62.5 1.1 copy-start.5
  65.6 2.1 copy-start.3
  67.7 142.1 %copy-start.4 = (f32[2,192,384]{2,1,0:T(8,128)}, f32[2,192,384]{2,1,0:T(8,128)S(1)}, u32[]{:S(2)}) copy-start(f32[2,192,384]{2,1,0:T(8,128)S(1)} %fusion.21) | copy-start | bytes 1769476
  71.3 113.9 %all-reduce.7.cloned.1.call-start = ((), (), s32[]{:S(2)}) async-start(), calls=%async_computation.1 | async-start | bytes 1179648 | tf_op jit(solution)/shard_map/psum | solution.py:58
Sparse Core Ops, SparseCore 0:
  71.4 37.0 all-reduce.4
  111.9 73.2 all-reduce.6
